TPU v7x, 32 devices: a whole 2x2x4 slice. The times are simulated.
32 devices in a mesh: tm: 16 (over z, y, x), space: 2 (over core).
Axes of the slice: x: 2, y: 2, z: 4, core: 2. Of those that a mesh axis runs over, the one named last changes fastest.
Arguments:
- features: bfloat16 [16, 16, 16, 256], P('tm', 'space'), may hold values from -6 to 6
- masks: int32 [16, 16, 16], P('tm', 'space'), may hold values from 0 to 1
- w_pix: bfloat16 [256, 256], replicated, may hold values from -0.375 to 0.375
- mask_embed: bfloat16 [256], replicated, may hold values from -4 to 4
- w_conv: bfloat16 [3, 3, 256, 256], replicated, may hold values from -0.125 to 0.125
- w_out: bfloat16 [256, 64], replicated, may hold values from -0.375 to 0.375
- w_ptr: bfloat16 [256, 256], replicated, may hold values from -0.375 to 0.375
- w_query: bfloat16 [256, 256], replicated, may hold values from -1 to 1
- w_key: bfloat16 [64, 256], replicated, may hold values from -0.75 to 0.75
- w_value: bfloat16 [64, 256], replicated, may hold values from -0.75 to 0.75
- w_proj: bfloat16 [256, 256], replicated, may hold values from -0.375 to 0.375
- mem_tpos: bfloat16 [3, 64], replicated, may hold values from -120 to 120
- ptr_tpos: bfloat16 [16, 256], replicated, may hold values from -4 to 4
- empty_memory: bfloat16 [64], replicated, may hold values from -4 to 4
Outputs:
- attended: bfloat16 [16, 16, 16, 256], P('tm', 'space')
- memory: bfloat16 [16, 16, 1024], P('tm', 'space')
- pointers: bfloat16 [16, 256], P('tm')
All inputs are finite; a program needn't handle non-finite values.
Results may differ from a plain program's by a relative error of at most 0.015.
The roundings to bfloat16 on the way count: a program that leaves them out, or rounds other values in their place, can miss the bound.
Values may be sent and summed in bfloat16 or wider, within the bound.
A program may use at most 128 MiB of HBM per device.

v0:
```python
import jax
import jax.numpy as jnp
from jax import lax
from jax.sharding import PartitionSpec as P

MEMS = 3
POINTERS = 16


def from_behind(block, axis, distance):
    devices = range(lax.axis_size(axis))
    route = [(i - distance, i) for i in devices if i - distance in devices]
    return lax.ppermute(block, axis, route)


def with_halo(block, sides, width):
    for axis, dim in sides:
        count = lax.axis_size(axis)
        forward = [(i, i + 1) for i in range(count - 1)]
        backward = [(target, source) for source, target in forward]
        low = lax.ppermute(
            lax.slice_in_dim(block, block.shape[dim] - width, None, axis=dim), axis, forward
        )
        high = lax.ppermute(lax.slice_in_dim(block, 0, width, axis=dim), axis, backward)
        block = jnp.concatenate([low, block, high], axis=dim)
    return block


def fetch_earlier(carried, hop_count):
    pieces = []
    for step_index in range(hop_count):
        pieces.append(from_behind(carried, "tm", step_index + 1))
    return jnp.concatenate(pieces[::-1], axis=0)


def attend(query, blocks):
    scores = []
    row_top = None
    for key_rows, value_rows, is_valid in blocks:
        block_scores = lax.dot_general(
            query, key_rows, (((1,), (1,)), ((), ())), preferred_element_type=jnp.float32
        )
        block_scores = jnp.where(is_valid, block_scores, -jnp.inf)
        scores.append(block_scores)
        block_top = jnp.max(block_scores, axis=1, keepdims=True)
        row_top = block_top if row_top is None else jnp.maximum(row_top, block_top)
    row_total = jnp.zeros_like(row_top)
    for block_scores in scores:
        row_total = row_total + jnp.sum(jnp.exp(block_scores - row_top), axis=1, keepdims=True)
    mixed_sum = jnp.zeros((query.shape[0], blocks[0][1].shape[1]), jnp.float32)
    for block_scores, block in zip(scores, blocks):
        weights = (jnp.exp(block_scores - row_top) / row_total).astype(jnp.bfloat16)
        mixed_sum = mixed_sum + jnp.dot(weights, block[1], preferred_element_type=jnp.float32)
    return mixed_sum.astype(jnp.bfloat16)


def body(
    features,
    masks,
    w_pix,
    mask_embed,
    w_conv,
    w_out,
    w_ptr,
    w_query,
    w_key,
    w_value,
    w_proj,
    mem_tpos,
    ptr_tpos,
    empty_memory,
):
    frames_dev, rows_dev, columns, model_dim = features.shape
    mem_dim = w_key.shape[0]
    ptr_tok = model_dim // mem_dim
    band_tokens = rows_dev * columns
    flat_rows = features.reshape(frames_dev * band_tokens, model_dim)
    mask_rows = masks.reshape(frames_dev * band_tokens, 1).astype(jnp.float32)
    joined_map = (
        jnp.dot(flat_rows, w_pix, preferred_element_type=jnp.float32)
        + mask_rows * mask_embed.astype(jnp.float32)
    ).astype(jnp.bfloat16)
    joined_map = joined_map.reshape(frames_dev, rows_dev, columns, model_dim)
    padded = with_halo(joined_map, (("space", 1),), 1)
    padded = jnp.pad(padded, ((0, 0), (0, 0), (1, 1), (0, 0)))
    conv_sum = jnp.zeros((frames_dev * band_tokens, model_dim), jnp.float32)
    for row_tap in range(3):
        for col_tap in range(3):
            window_rows = padded[
                :, row_tap : row_tap + rows_dev, col_tap : col_tap + columns, :
            ].reshape(-1, model_dim)
            conv_sum = conv_sum + jnp.dot(
                window_rows, w_conv[row_tap, col_tap], preferred_element_type=jnp.float32
            )
    hidden = jax.nn.gelu(conv_sum, approximate=True).astype(jnp.bfloat16)
    memory = jnp.dot(hidden, w_out, preferred_element_type=jnp.float32).astype(jnp.bfloat16)
    memory = memory.reshape(frames_dev, rows_dev, columns * mem_dim)
    band_mask = masks.reshape(frames_dev, band_tokens).astype(jnp.bfloat16)
    partial_value = jnp.einsum(
        "ft,ftd->fd",
        band_mask,
        features.reshape(frames_dev, band_tokens, model_dim),
        preferred_element_type=jnp.float32,
    )
    pooled = lax.psum(partial_value, "space")
    normed = (pooled * lax.rsqrt(jnp.mean(pooled * pooled, axis=1, keepdims=True) + 1e-06)).astype(
        jnp.bfloat16
    )
    pointers = jnp.dot(normed, w_ptr, preferred_element_type=jnp.float32).astype(jnp.bfloat16)
    all_pointers = lax.all_gather(pointers, "tm", axis=0, tiled=True)
    hop_count = (MEMS + frames_dev - 1) // frames_dev
    carried = lax.all_gather(memory, "space", axis=1, tiled=True)
    history = jnp.concatenate(
        [fetch_earlier(carried, hop_count), carried[: frames_dev - 1]], axis=0
    )
    grid_tokens = columns * columns
    hist_frames = history.shape[0]
    history = history.reshape(hist_frames, grid_tokens, mem_dim)
    hist_values = jnp.dot(
        history.reshape(-1, mem_dim), w_value, preferred_element_type=jnp.float32
    ).astype(jnp.bfloat16)
    hist_values = hist_values.reshape(hist_frames, grid_tokens, model_dim)
    tpos_keys = jnp.dot(mem_tpos, w_key, preferred_element_type=jnp.float32)
    ptr_tpos_keys = jnp.dot(
        ptr_tpos[::-1].reshape(POINTERS * ptr_tok, mem_dim),
        w_key,
        preferred_element_type=jnp.float32,
    )
    null_key = jnp.dot(
        empty_memory.reshape(1, mem_dim), w_key, preferred_element_type=jnp.float32
    ).astype(jnp.bfloat16)
    null_value = jnp.dot(
        empty_memory.reshape(1, mem_dim), w_value, preferred_element_type=jnp.float32
    ).astype(jnp.bfloat16)
    padded_ptr = jnp.concatenate(
        [jnp.zeros((POINTERS, model_dim), jnp.bfloat16), all_pointers], axis=0
    )
    ptr_offsets = jnp.repeat(jnp.arange(POINTERS, dtype=jnp.int32) - POINTERS, ptr_tok)
    features_f = features.reshape(frames_dev, band_tokens, model_dim).astype(jnp.float32)
    first_frame = lax.axis_index("tm") * frames_dev
    frame = first_frame + 0
    rows_f = features_f[0]
    centred = rows_f - jnp.mean(rows_f, axis=1, keepdims=True)
    query_in = (
        centred * lax.rsqrt(jnp.mean(centred * centred, axis=1, keepdims=True) + 1e-05)
    ).astype(jnp.bfloat16)
    query = (
        jnp.dot(query_in, w_query, preferred_element_type=jnp.float32) * model_dim ** (-0.5)
    ).astype(jnp.bfloat16)
    blocks = []
    for distance in range(1, MEMS + 1):
        slot_index = hop_count * frames_dev - distance
        key_rows = (
            jnp.dot(history[slot_index], w_key, preferred_element_type=jnp.float32)
            + tpos_keys[distance - 1]
        ).astype(jnp.bfloat16)
        blocks.append((key_rows, hist_values[slot_index], frame - distance >= 0))
    window = lax.dynamic_slice_in_dim(padded_ptr, frame, POINTERS, 0)
    ptr_tokens = window.reshape(POINTERS * ptr_tok, mem_dim)
    ptr_keys = (
        jnp.dot(ptr_tokens, w_key, preferred_element_type=jnp.float32) + ptr_tpos_keys
    ).astype(jnp.bfloat16)
    ptr_values = jnp.dot(ptr_tokens, w_value, preferred_element_type=jnp.float32).astype(
        jnp.bfloat16
    )
    extra_valid = jnp.concatenate([frame + ptr_offsets >= 0, jnp.ones((1,), bool)], axis=0)
    blocks.append(
        (
            jnp.concatenate([ptr_keys, null_key], axis=0),
            jnp.concatenate([ptr_values, null_value], axis=0),
            extra_valid[None, :],
        )
    )
    mixed_rows = attend(query, blocks)
    outputs = [
        (rows_f + jnp.dot(mixed_rows, w_proj, preferred_element_type=jnp.float32)).astype(
            jnp.bfloat16
        )
    ]
    attended = jnp.stack(outputs, axis=0).reshape(frames_dev, rows_dev, columns, model_dim)
    return (attended, memory, pointers)


def solution(mesh):
    return jax.shard_map(
        body,
        mesh=mesh,
        in_specs=(
            P("tm", "space", None, None),
            P("tm", "space", None),
            P(),
            P(),
            P(),
            P(),
            P(),
            P(),
            P(),
            P(),
            P(),
            P(),
            P(),
            P(),
        ),
        out_specs=(P("tm", "space", None, None), P("tm", "space", None), P("tm", None)),
        check_vma=False,
    )
```

profile of v0, /device:TPU:24, one launch (start us, length us, event | category | flops | bytes accessed | tf_op | source)
XLA Modules:
  0.0 78.9 jit_solution(8171158523613113094)
XLA Ops:
  0.6 0.0 copy-start
  0.7 0.0 copy-start.7
  0.7 0.0 copy-start.4
  0.7 0.7 convert_element_type.111
  1.4 0.8 convert_bitcast_fusion
  2.2 0.1 convert_element_type.110
  2.3 1.0 %fusion.12 = bf16[128,256]{1,0:T(8,128)(2,1)S(1)} fusion(bf16[128,256]{1,0:T(8,128)(2,1)} %bitcast.107, bf16[256,256]{1,0:T(8,128)(2,1)S(1)} %copy-done, f32[256]{0:T(256)S(1)} %convert_element_type.111, f32[128]{0:T(128)S(1)} %convert_element_type.110), kind=kOutput, calls=%fused_computation.29 | convolution fusion | flops 16875520 | bytes 263680 | tf_op jit(solution)/shard_map/dot_general | solution.py:80
  3.3 1.3 %collective-permute-start.1 = (bf16[1,1,16,256]{3,2,1,0:T(8,128)(2,1)S(1)}, bf16[1,1,16,256]{3,2,1,0:T(8,128)(2,1)S(1)}, u32[]{:S(2)}, u32[]{:S(2)}) collective-permute-start(bf16[1,1,16,256]{3,2,1,0:T(8,128)(2,1)S(1)} %get-tuple-element.15), channel_id=1, source_target_pairs={{1,0},{3,2},{5,4},{7,6},{9,8},{11,10},{13,12},{15,14},{17,16},{19,... | collective-permute-start | bytes 24584 | tf_op jit(solution)/shard_map/ppermute | solution.py:24
  4.6 3.0 %collective-permute-start = (bf16[1,1,16,256]{3,2,1,0:T(8,128)(2,1)S(1)}, bf16[1,1,16,256]{3,2,1,0:T(8,128)(2,1)S(1)}, u32[]{:S(2)}, u32[]{:S(2)}) collective-permute-start(bf16[1,1,16,256]{3,2,1,0:T(8,128)(2,1)S(1)} %get-tuple-element.14), channel_id=1, source_target_pairs={{0,1},{2,3},{4,5},{6,7},{8,9},{10,11},{12,13},{14,15},{16,17},{18,... | collective-permute-start | bytes 24584 | tf_op jit(solution)/shard_map/ppermute | solution.py:21
  7.6 0.9 %convert_reduce_fusion = f32[8,16]{1,0:T(8,128)S(1)} fusion(bf16[1,8,16,256]{3,2,1,0:T(8,128)(2,1)} %param.14), kind=kLoop, calls=%fused_computation.42 | loop fusion | flops 65408 | bytes 66048 | tf_op jit(solution)/shard_map/reduce_sum | solution.py:143
  8.6 1.1 %fusion.22 = f32[8,16]{1,0:T(8,128)S(1)} fusion(bf16[1,8,16,256]{3,2,1,0:T(8,128)(2,1)} %param.14, f32[8,16]{1,0:T(8,128)S(1)} %broadcast_multiply_fusion), kind=kLoop, calls=%fused_computation.50 | loop fusion | flops 130944 | bytes 66560 | tf_op jit(solution)/shard_map/reduce_sum | solution.py:145
  9.7 0.1 div.40
  9.8 0.1 rsqrt.16
  9.8 0.9 %fusion.117 = f32[3,256]{1,0:T(4,128)S(1)} fusion(bf16[3,64]{1,0:T(4,128)(2,1)} %param.25, bf16[64,256]{1,0:T(8,128)(2,1)} %param.22), kind=kOutput, calls=%fused_computation.157 | convolution fusion | flops 98304 | bytes 36224 | tf_op jit(solution)/shard_map/dot_general | solution.py:123
  10.8 0.9 %fusion.100 = f32[1,256]{1,0:T(1,128)S(1)} fusion(bf16[64,256]{1,0:T(8,128)(2,1)} %param.22, bf16[64]{0:T(256)(128)(2,1)} %param.27), kind=kOutput, calls=%fused_computation.138 | convolution fusion | flops 32768 | bytes 33920 | tf_op jit(solution)/shard_map/dot_general | solution.py:129
  11.7 1.0 %convolution_bitcast_fusion = f32[1,256]{1,0:T(1,128)S(1)} fusion(bf16[1,8,16,256]{3,2,1,0:T(8,128)(2,1)} %param.14, bf16[8,16,1]{1,0,2:T(8,128)(2,1)S(1)} %get-tuple-element.19), kind=kOutput, calls=%fused_computation.36 | convolution fusion | flops 65536 | bytes 66816 | tf_op jit(solution)/shard_map/ft,ftd->fd/dot_general | solution.py:99
  12.7 2.4 %psum.7 = f32[1,256]{1,0:T(1,128)S(1)} all-reduce(f32[1,256]{1,0:T(1,128)S(1)} %convolution_bitcast_fusion), channel_id=1, replica_groups=mesh['tm'=16,'space'=2] {'space'}, use_global_device_ids=true, to_apply=%region_5.6 | all-reduce | flops 256 | bytes 2048 | tf_op jit(solution)/shard_map/psum | solution.py:105
  15.2 0.6 multiply_reduce_fusion
  16.5 1.0 %fusion.94 = f32[1,256]{1,0:T(1,128)S(1)} fusion(bf16[256,256]{1,0:T(8,128)(2,1)} %param.20, f32[1,256]{1,0:T(1,128)S(1)} %psum.7, f32[]{:T(128)S(6)} %rsqrt.17), kind=kOutput, calls=%fused_computation.131 | convolution fusion | flops 131584 | bytes 133124 | tf_op jit(solution)/shard_map/dot_general | solution.py:109
  17.5 32.6 %all-gather.1 = bf16[16,1,256]{2,1,0:T(2,128)(2,1)S(1)} all-gather(bf16[1,1,256]{2,1,0:T(2,128)(2,1)S(1)} %reshape.203), channel_id=2, replica_groups=mesh['tm'=16,'space'=2] {'tm'}, dimensions={0}, use_global_device_ids=true | all-gather | bytes 8704 | tf_op jit(solution)/shard_map/all_gather | solution.py:110
  50.1 0.1 reshape.200
  50.2 0.9 %fusion.118 = f32[64,256]{1,0:T(8,128)S(1)} fusion(bf16[64,64]{1,0:T(8,128)(2,1)S(1)} %reshape.200, bf16[64,256]{1,0:T(8,128)(2,1)} %param.22), kind=kOutput, calls=%fused_computation.158 | convolution fusion | flops 2097152 | bytes 106496 | tf_op jit(solution)/shard_map/dot_general | solution.py:161
  51.1 0.7 rev.3
  51.8 0.1 reshape.201
  51.9 0.1 broadcast_in_dim.21
  52.0 0.1 ge.24
  52.1 0.9 %convolution_convert_fusion.1 = bf16[64,256]{1,0:T(8,128)(2,1)S(1)} fusion(bf16[64,64]{1,0:T(8,128)(2,1)S(1)} %reshape.200, bf16[64,256]{1,0:T(8,128)(2,1)} %param.23), kind=kOutput, calls=%fused_computation.33 | convolution fusion | flops 2113536 | bytes 73728 | tf_op jit(solution)/shard_map/dot_general | solution.py:163
  53.0 0.9 %fusion.14 = bf16[64,256]{1,0:T(8,128)(2,1)S(1)} fusion(f32[64,256]{1,0:T(8,128)S(1)} %fusion.118, bf16[64,64]{1,0:T(8,128)(2,1)S(1)} %reshape.201, bf16[64,256]{1,0:T(8,128)(2,1)} %param.22), kind=kOutput, calls=%fused_computation.32 | convolution fusion | flops 2129920 | bytes 139264 | tf_op jit(solution)/shard_map/dot_general | solution.py:124
  53.9 0.1 pad_add_fusion
  54.0 0.2 fusion.11
  54.2 0.2 fusion.113
  54.4 0.1 fusion.98
  54.6 0.2 fusion.35
  54.8 0.2 fusion.45
  55.0 0.2 convolution_add_fusion.13
  55.1 0.2 convolution_add_fusion.12
  55.3 0.2 convolution_add_fusion.11
  55.5 0.2 convolution_add_fusion.10
  55.7 0.2 convolution_add_fusion.9
  55.8 0.2 convolution_add_fusion.8
  56.0 0.3 convolution_convert_fusion.2
  56.4 0.1 copy.19
  56.5 0.1 reshape.196
  56.6 0.0 copy-start.6
  56.6 1.8 %all_gather.6 = bf16[1,16,1024]{2,1,0:T(8,128)(2,1)S(1)} all-gather(bf16[1,8,1024]{2,1,0:T(8,128)(2,1)S(1)} %reshape.196), channel_id=1, replica_groups=mesh['tm'=16,'space'=2] {'space'}, dimensions={1}, use_global_device_ids=true | all-gather | bytes 49152 | tf_op jit(solution)/shard_map/all_gather | solution.py:112
  58.4 3.4 %collective-permute-start.2 = (bf16[1,16,1024]{2,1,0:T(8,128)(2,1)S(1)}, bf16[1,16,1024]{2,1,0:T(8,128)(2,1)S(1)}, u32[]{:S(2)}, u32[]{:S(2)}) collective-permute-start(bf16[1,16,1024]{2,1,0:T(8,128)(2,1)S(1)} %all_gather.6), channel_id=1, source_target_pairs={{0,2},{2,4},{4,6},{6,8},{8,10},{10,12},{12,14},{14,16},{16,18},{18... | collective-permute-start | bytes 98312 | tf_op jit(solution)/shard_map/ppermute | solution.py:13
  61.9 6.1 %collective-permute-start.3 = (bf16[1,16,1024]{2,1,0:T(8,128)(2,1)S(1)}, bf16[1,16,1024]{2,1,0:T(8,128)(2,1)S(1)}, u32[]{:S(2)}, u32[]{:S(2)}) collective-permute-start(bf16[1,16,1024]{2,1,0:T(8,128)(2,1)S(1)} %all_gather.6), channel_id=1, source_target_pairs={{0,4},{2,6},{4,8},{6,10},{8,12},{10,14},{12,16},{14,18},{16,20},{1... | collective-permute-start | bytes 98312 | tf_op jit(solution)/shard_map/ppermute | solution.py:13
  68.0 1.9 %collective-permute-start.4 = (bf16[1,16,1024]{2,1,0:T(8,128)(2,1)S(1)}, bf16[1,16,1024]{2,1,0:T(8,128)(2,1)S(1)}, u32[]{:S(2)}, u32[]{:S(2)}) collective-permute-start(bf16[1,16,1024]{2,1,0:T(8,128)(2,1)S(1)} %all_gather.6), channel_id=1, source_target_pairs={{0,6},{2,8},{4,10},{6,12},{8,14},{10,16},{12,18},{14,20},{16,22},{... | collective-permute-start | bytes 98312 | tf_op jit(solution)/shard_map/ppermute | solution.py:13
  69.9 0.6 convert_element_type.121
  70.5 4.2 %collective-permute-done.4 = bf16[1,16,1024]{2,1,0:T(8,128)(2,1)S(1)} collective-permute-done((bf16[1,16,1024]{2,1,0:T(8,128)(2,1)S(1)}, bf16[1,16,1024]{2,1,0:T(8,128)(2,1)S(1)}, u32[]{:S(2)}, u32[]{:S(2)}) %collective-permute-start.4) | collective-permute-done | bytes 32800 | tf_op jit(solution)/shard_map/ppermute | solution.py:13
  74.7 0.2 reshape_reshape.3
  74.9 0.2 convolution_convert_fusion
  75.1 0.1 squeeze.49
  75.2 0.4 fusion.115
  75.6 0.1 squeeze.51
  75.8 0.4 fusion.114
  76.2 0.1 squeeze.50
  76.3 0.4 fusion.116
  76.8 0.2 fusion.63
  77.1 0.2 fusion.33
  77.3 0.2 convolution_add_fusion.6
  77.5 0.2 convolution_add_fusion.5
  77.8 0.2 copy-done.5
  78.0 1.0 %fusion.13 = bf16[128,256]{1,0:T(8,128)(2,1)} fusion(bf16[256,256]{1,0:T(8,128)(2,1)S(1)} %copy-done.5, f32[128,256]{1,0:T(8,128)S(1)} %convolution_add_fusion.5, bf16[128,256]{1,0:T(8,128)(2,1)S(1)} %bitcast.109, bf16[1,256]{1,0:T(2,128)(2,1)S(1)} %convert_element_type.132, bf16[64,256]{1,0:T(8,128)(2,1)S(1)} %convolution_convert_fusion.1, ...), kind=kOutput, calls=%fused_computation.30 | convolution fusion | flops 21292416 | bytes 460800 | tf_op jit(solution)/shard_map/dot_general | solution.py:176
  (39 shorter events, 0.3 us)
Async XLA Ops:
  0.6 1.6 %copy-start = (bf16[256,256]{1,0:T(8,128)(2,1)S(1)}, bf16[256,256]{1,0:T(8,128)(2,1)}, u32[]{:S(2)}) copy-start(bf16[256,256]{1,0:T(8,128)(2,1)} %param.16) | copy-start | bytes 393220
  0.6 53.3 %copy-start.2 = (bf16[1,8,16,256]{3,2,1,0:T(8,128)(2,1)S(1)}, bf16[1,8,16,256]{3,2,1,0:T(8,128)(2,1)}, u32[]{:S(2)}) copy-start(bf16[1,8,16,256]{3,2,1,0:T(8,128)(2,1)} %param.14) | copy-start | bytes 196612
  0.7 53.7 %copy-start.7 = (bf16[64]{0:T(256)(128)(2,1)S(1)}, bf16[64]{0:T(256)(128)(2,1)}, u32[]{:S(2)}) copy-start(bf16[64]{0:T(256)(128)(2,1)} %param.27) | copy-start | bytes 388
  0.7 53.7 %copy-start.4 = (bf16[64,256]{1,0:T(8,128)(2,1)S(1)}, bf16[64,256]{1,0:T(8,128)(2,1)}, u32[]{:S(2)}) copy-start(bf16[64,256]{1,0:T(8,128)(2,1)} %param.23) | copy-start | bytes 98308
  0.7 53.3 %copy-start.8 = (bf16[256,256]{1,0:T(8,128)(2,1)S(1)}, bf16[256,256]{1,0:T(8,128)(2,1)}, u32[]{:S(2)}) copy-start(bf16[256,256]{1,0:T(8,128)(2,1)} %param.21) | copy-start | bytes 393220
  3.3 51.2 %collective-permute-start.1 = (bf16[1,1,16,256]{3,2,1,0:T(8,128)(2,1)S(1)}, bf16[1,1,16,256]{3,2,1,0:T(8,128)(2,1)S(1)}, u32[]{:S(2)}, u32[]{:S(2)}) collective-permute-start(bf16[1,1,16,256]{3,2,1,0:T(8,128)(2,1)S(1)} %get-tuple-element.15), channel_id=1, source_target_pairs={{1,0},{3,2},{5,4},{7,6},{9,8},{11,10},{13,12},{15,14},{17,16},{19,... | collective-permute-start | bytes 24584 | tf_op jit(solution)/shard_map/ppermute | solution.py:24
  4.6 49.9 %collective-permute-start = (bf16[1,1,16,256]{3,2,1,0:T(8,128)(2,1)S(1)}, bf16[1,1,16,256]{3,2,1,0:T(8,128)(2,1)S(1)}, u32[]{:S(2)}, u32[]{:S(2)}) collective-permute-start(bf16[1,1,16,256]{3,2,1,0:T(8,128)(2,1)S(1)} %get-tuple-element.14), channel_id=1, source_target_pairs={{0,1},{2,3},{4,5},{6,7},{8,9},{10,11},{12,13},{14,15},{16,17},{18,... | collective-permute-start | bytes 24584 | tf_op jit(solution)/shard_map/ppermute | solution.py:21
  8.6 46.0 %copy-start.3 = (bf16[3,3,256,256]{3,2,1,0:T(8,128)(2,1)S(1)}, bf16[3,3,256,256]{3,2,1,0:T(8,128)(2,1)}, u32[]{:S(2)}) copy-start(bf16[3,3,256,256]{3,2,1,0:T(8,128)(2,1)} %param.18) | copy-start | bytes 3538948
  55.1 0.9 %copy-start.9 = (bf16[256,64]{0,1:T(8,128)(2,1)S(1)}, bf16[256,64]{0,1:T(8,128)(2,1)}, u32[]{:S(2)}) copy-start(bf16[256,64]{0,1:T(8,128)(2,1)} %param.19) | copy-start | bytes 98308
  55.8 19.4 %copy-start.1 = (bf16[64,256]{1,0:T(8,128)(2,1)S(1)}, bf16[64,256]{1,0:T(8,128)(2,1)}, u32[]{:S(2)}) copy-start(bf16[64,256]{1,0:T(8,128)(2,1)} %param.22) | copy-start | bytes 98308
  56.6 20.2 %copy-start.6 = (bf16[1,8,1024]{2,1,0:T(8,128)(2,1)}, bf16[1,8,1024]{2,1,0:T(8,128)(2,1)S(1)}, u32[]{:S(2)}) copy-start(bf16[1,8,1024]{2,1,0:T(8,128)(2,1)S(1)} %reshape.196) | copy-start | bytes 49156
  58.4 12.0 %collective-permute-start.2 = (bf16[1,16,1024]{2,1,0:T(8,128)(2,1)S(1)}, bf16[1,16,1024]{2,1,0:T(8,128)(2,1)S(1)}, u32[]{:S(2)}, u32[]{:S(2)}) collective-permute-start(bf16[1,16,1024]{2,1,0:T(8,128)(2,1)S(1)} %all_gather.6), channel_id=1, source_target_pairs={{0,2},{2,4},{4,6},{6,8},{8,10},{10,12},{12,14},{14,16},{16,18},{18... | collective-permute-start | bytes 98312 | tf_op jit(solution)/shard_map/ppermute | solution.py:13
  61.9 8.6 %collective-permute-start.3 = (bf16[1,16,1024]{2,1,0:T(8,128)(2,1)S(1)}, bf16[1,16,1024]{2,1,0:T(8,128)(2,1)S(1)}, u32[]{:S(2)}, u32[]{:S(2)}) collective-permute-start(bf16[1,16,1024]{2,1,0:T(8,128)(2,1)S(1)} %all_gather.6), channel_id=1, source_target_pairs={{0,4},{2,6},{4,8},{6,10},{8,12},{10,14},{12,16},{14,18},{16,20},{1... | collective-permute-start | bytes 98312 | tf_op jit(solution)/shard_map/ppermute | solution.py:13
  68.0 6.7 %collective-permute-start.4 = (bf16[1,16,1024]{2,1,0:T(8,128)(2,1)S(1)}, bf16[1,16,1024]{2,1,0:T(8,128)(2,1)S(1)}, u32[]{:S(2)}, u32[]{:S(2)}) collective-permute-start(bf16[1,16,1024]{2,1,0:T(8,128)(2,1)S(1)} %all_gather.6), channel_id=1, source_target_pairs={{0,6},{2,8},{4,10},{6,12},{8,14},{10,16},{12,18},{14,20},{16,22},{... | collective-permute-start | bytes 98312 | tf_op jit(solution)/shard_map/ppermute | solution.py:13
  77.0 0.9 %copy-start.5 = (bf16[256,256]{1,0:T(8,128)(2,1)S(1)}, bf16[256,256]{1,0:T(8,128)(2,1)}, u32[]{:S(2)}) copy-start(bf16[256,256]{1,0:T(8,128)(2,1)} %param.24) | copy-start | bytes 393220
where the time goes:
time: 79.8 us; the launch traced here: 78.9 us
  blocking collectives  36.9 us (46%)
  starting transfers between devices  15.7 us (20%)
  matrix products  12.9 us (16%)
  other arithmetic  4.59 us (6%)
  waiting for transfers between devices  4.19 us (5%)
  local copies, waits for them, and re-layouts  2.96 us (4%)
  between operations  1.72 us (2%)
    all_gather x1, blocking collectives, body(): all_pointers = lax.all_gather(pointers, 'tm', axis=0, tiled=True)  32.6 us
    ppermute x3, starting transfers between devices, from_behind(): return lax.ppermute(block, axis, route)  11.4 us
    ppermute x3, waiting for transfers between devices, from_behind(): return lax.ppermute(block, axis, route)  4.18 us
    ppermute x1, starting transfers between devices, with_halo(): lax.ppermute(lax.slice_in_dim(block, block.shape[dim] - width, None, axis...  3.03 us
    psum x1, blocking collectives, body(): pooled = lax.psum(partial_value, 'space')  2.45 us
    all_gather x1, blocking collectives, body(): carried = lax.all_gather(memory, 'space', axis=1, tiled=True)  1.83 us
  transfers between devices with their start and end apart: 5, of which 1 were waited for; matrix products, arithmetic and copies ran while one was open for 15% of the time, Pallas kernels for 0%

commit v1 on v0

--- a/solution.py
+++ b/solution.py
@@ -107,7 +107,15 @@
         jnp.bfloat16
     )
     pointers = jnp.dot(normed, w_ptr, preferred_element_type=jnp.float32).astype(jnp.bfloat16)
-    all_pointers = lax.all_gather(pointers, "tm", axis=0, tiled=True)
+    all_pointers = jnp.concatenate(
+        lax.all_to_all(
+            jnp.stack([pointers for _ in range(lax.axis_size("tm"))]),
+            axis_name="tm",
+            split_axis=0,
+            concat_axis=0,
+        ),
+        axis=0,
+    )
     hop_count = (MEMS + frames_dev - 1) // frames_dev
     carried = lax.all_gather(memory, "space", axis=1, tiled=True)
     history = jnp.concatenate(

time: 79.8 us -> 52.9 us (0.66)
  the two profiles are of different devices: /device:TPU:24 before, /device:TPU:10 now
where the time goes in v1:
time: 52.9 us; the launch traced here: 52.2 us
  starting transfers between devices  21.6 us (41%)
  matrix products  12.3 us (23%)
  other arithmetic  5.23 us (10%)
  blocking collectives  4.28 us (8%)
  waiting for transfers between devices  3.49 us (7%)
  local copies, waits for them, and re-layouts  3.48 us (7%)
  between operations  1.74 us (3%)
    ppermute x3, starting transfers between devices, from_behind(): return lax.ppermute(block, axis, route)  10.1 us
    all_to_all x1, starting transfers between devices, body(): lax.all_to_all(jnp.stack([pointers for _ in range(lax.axis_size('tm'))]),...  7.2 us
    ppermute x3, waiting for transfers between devices, from_behind(): return lax.ppermute(block, axis, route)  3.49 us
    ppermute x1, starting transfers between devices, with_halo(): lax.ppermute(lax.slice_in_dim(block, block.shape[dim] - width, None, axis...  3.03 us
    psum x1, blocking collectives, body(): pooled = lax.psum(partial_value, 'space')  2.45 us
    all_gather x1, blocking collectives, body(): carried = lax.all_gather(memory, 'space', axis=1, tiled=True)  1.83 us
    dot_general x4, matrix products, attend(): lax.dot_general(query, key_rows, (((1,), (1,)), ((), ())), preferred_elem...  1.45 us
    dot_general x8, matrix products, body(): jnp.dot(window_rows, w_conv[row_tap, col_tap], preferred_element_type=jnp...  1.32 us
  transfers between devices with their start and end apart: 6, of which 1 were waited for; matrix products, arithmetic and copies ran while one was open for 27% of the time, Pallas kernels for 0%

profile of v1, /device:TPU:10, one launch (start us, length us, event | category | flops | bytes accessed | tf_op | source)
XLA Modules:
  0.0 52.2 jit_solution(10470926022673179398)
XLA Ops:
  0.7 0.8 %convert_element_type.111 = f32[256]{0:T(256)S(1)} convert(bf16[256]{0:T(256)(128)(2,1)} %param.17) | non-fusion elementwise | flops 256 | bytes 1536 | tf_op jit(solution)/shard_map/convert_element_type | solution.py:81
  1.4 0.8 %convert_bitcast_fusion = (bf16[8,16,1]{1,0,2:T(8,128)(2,1)S(1)}, f32[1,8,16]{2,1,0:T(8,128)S(1)}) fusion(s32[1,8,16]{2,1,0:T(8,128)} %param.15), kind=kLoop, calls=%fused_computation.128 | loop fusion | flops 256 | bytes 1280 | tf_op jit(solution)/shard_map/reshape.135
  2.2 0.1 convert_element_type.110
  2.3 1.0 %fusion.12 = bf16[128,256]{1,0:T(8,128)(2,1)S(1)} fusion(bf16[128,256]{1,0:T(8,128)(2,1)} %bitcast.107, bf16[256,256]{1,0:T(8,128)(2,1)S(1)} %copy-done, f32[256]{0:T(256)S(1)} %convert_element_type.111, f32[128]{0:T(128)S(1)} %convert_element_type.110), kind=kOutput, calls=%fused_computation.29 | convolution fusion | flops 16875520 | bytes 263680 | tf_op jit(solution)/shard_map/dot_general | solution.py:80
  3.3 1.3 %collective-permute-start.1 = (bf16[1,1,16,256]{3,2,1,0:T(8,128)(2,1)S(1)}, bf16[1,1,16,256]{3,2,1,0:T(8,128)(2,1)S(1)}, u32[]{:S(2)}, u32[]{:S(2)}) collective-permute-start(bf16[1,1,16,256]{3,2,1,0:T(8,128)(2,1)S(1)} %get-tuple-element.15), channel_id=1, source_target_pairs={{1,0},{3,2},{5,4},{7,6},{9,8},{11,10},{13,12},{15,14},{17,16},{19,... | collective-permute-start | bytes 24584 | tf_op jit(solution)/shard_map/ppermute | solution.py:24
  4.6 3.0 %collective-permute-start = (bf16[1,1,16,256]{3,2,1,0:T(8,128)(2,1)S(1)}, bf16[1,1,16,256]{3,2,1,0:T(8,128)(2,1)S(1)}, u32[]{:S(2)}, u32[]{:S(2)}) collective-permute-start(bf16[1,1,16,256]{3,2,1,0:T(8,128)(2,1)S(1)} %get-tuple-element.14), channel_id=1, source_target_pairs={{0,1},{2,3},{4,5},{6,7},{8,9},{10,11},{12,13},{14,15},{16,17},{18,... | collective-permute-start | bytes 24584 | tf_op jit(solution)/shard_map/ppermute | solution.py:21
  7.6 1.0 %convolution_bitcast_fusion = f32[1,256]{1,0:T(1,128)S(1)} fusion(bf16[1,8,16,256]{3,2,1,0:T(8,128)(2,1)} %param.14, bf16[8,16,1]{1,0,2:T(8,128)(2,1)S(1)} %get-tuple-element.19), kind=kOutput, calls=%fused_computation.36 | convolution fusion | flops 65536 | bytes 66816 | tf_op jit(solution)/shard_map/ft,ftd->fd/dot_general | solution.py:99
  8.7 2.4 %psum.7 = f32[1,256]{1,0:T(1,128)S(1)} all-reduce(f32[1,256]{1,0:T(1,128)S(1)} %convolution_bitcast_fusion), channel_id=1, replica_groups=mesh['tm'=16,'space'=2] {'space'}, use_global_device_ids=true, to_apply=%region_5.6 | all-reduce | flops 256 | bytes 2048 | tf_op jit(solution)/shard_map/psum | solution.py:105
  11.1 0.6 %multiply_reduce_fusion = f32[]{:T(128)} fusion(f32[1,256]{1,0:T(1,128)S(1)} %psum.7), kind=kLoop, calls=%fused_computation.135 | loop fusion | flops 511 | bytes 1028 | tf_op jit(solution)/shard_map/reduce_sum | solution.py:106
  12.4 1.0 %fusion.94 = f32[1,256]{1,0:T(1,128)S(1)} fusion(bf16[256,256]{1,0:T(8,128)(2,1)} %param.20, f32[1,256]{1,0:T(1,128)S(1)} %psum.7, f32[]{:T(128)S(6)} %rsqrt.17), kind=kOutput, calls=%fused_computation.131 | convolution fusion | flops 131584 | bytes 133124 | tf_op jit(solution)/shard_map/dot_general | solution.py:109
  13.5 0.5 broadcast.68
  14.0 0.7 %reduce.3 = bf16[16,256]{1,0:T(8,128)(2,1)S(1)} reduce(bf16[16,1,256]{2,1,0:T(2,128)(2,1)S(1)} %stack.2, bf16[]{:T(256)} %broadcast.68), dimensions={1}, to_apply=%stack.2.reduce_sub_computation | reduce | bytes 16386 | tf_op jit(solution)/shard_map/stack | solution.py:112
  14.7 0.6 %reshape.218 = bf16[16,2,128]{2,1,0:T(2,128)(2,1)} reshape(bf16[16,256]{1,0:T(8,128)(2,1)S(1)} %reduce.3) | data formatting | bytes 16384
  15.3 7.2 %all-to-all-start = ((bf16[16,2,128]{2,1,0:T(2,128)(2,1)}), bf16[16,2,128]{2,1,0:T(2,128)(2,1)S(1)}, u32[]{:S(2)}, u32[]{:S(2)}) async-start(bf16[16,2,128]{2,1,0:T(2,128)(2,1)} %reshape.218), calls=%async_computation | async-start | bytes 16384 | tf_op jit(solution)/shard_map/all_to_all | solution.py:111
  22.5 0.9 %convert_reduce_fusion = f32[8,16]{1,0:T(8,128)S(1)} fusion(bf16[1,8,16,256]{3,2,1,0:T(8,128)(2,1)} %param.14), kind=kLoop, calls=%fused_computation.42 | loop fusion | flops 65408 | bytes 66048 | tf_op jit(solution)/shard_map/reduce_sum | solution.py:151
  23.4 1.0 %fusion.22 = f32[8,16]{1,0:T(8,128)S(1)} fusion(bf16[1,8,16,256]{3,2,1,0:T(8,128)(2,1)} %param.14, f32[8,16]{1,0:T(8,128)S(1)} %broadcast_multiply_fusion), kind=kLoop, calls=%fused_computation.50 | loop fusion | flops 130944 | bytes 66560 | tf_op jit(solution)/shard_map/reduce_sum | solution.py:153
  24.5 0.1 div.40
  24.5 0.1 rsqrt.16
  24.6 0.9 %fusion.117 = f32[3,256]{1,0:T(4,128)S(1)} fusion(bf16[3,64]{1,0:T(4,128)(2,1)} %param.25, bf16[64,256]{1,0:T(8,128)(2,1)} %param.22), kind=kOutput, calls=%fused_computation.157 | convolution fusion | flops 98304 | bytes 36224 | tf_op jit(solution)/shard_map/dot_general | solution.py:131
  25.5 0.9 %fusion.100 = f32[1,256]{1,0:T(1,128)S(1)} fusion(bf16[64,256]{1,0:T(8,128)(2,1)} %param.22, bf16[64]{0:T(256)(128)(2,1)} %param.27), kind=kOutput, calls=%fused_computation.138 | convolution fusion | flops 32768 | bytes 33920 | tf_op jit(solution)/shard_map/dot_general | solution.py:137
  26.4 0.1 broadcast_in_dim.21
  26.5 0.1 ge.24
  26.6 0.9 %fusion.98 = f32[1,256]{1,0:T(1,128)S(1)} fusion(bf16[64,256]{1,0:T(8,128)(2,1)} %param.23, bf16[64]{0:T(256)(128)(2,1)} %param.27), kind=kOutput, calls=%fused_computation.136 | convolution fusion | flops 32768 | bytes 33920 | tf_op jit(solution)/shard_map/dot_general | solution.py:140
  27.5 1.2 %fusion.11 = bf16[128,256]{1,0:T(8,128)(2,1)S(1)} fusion(bf16[256,256]{1,0:T(8,128)(2,1)} %param.21, bf16[128,256]{1,0:T(8,128)(2,1)} %bitcast.108, f32[128]{0:T(128)S(1)} %rsqrt.16, f32[128]{0:T(128)S(1)} %div.40), kind=kOutput, calls=%fused_computation.28 | convolution fusion | flops 16973824 | bytes 263168 | tf_op jit(solution)/shard_map/dot_general | solution.py:156
  28.7 0.1 pad_add_fusion
  28.8 0.6 %convert_element_type.134 = bf16[1,256]{1,0:T(2,128)(2,1)} reshape(bf16[256]{0:T(256)(128)(2,1)S(1)} %convert_element_type.120) | data formatting | bytes 1024 | tf_op jit(solution)/shard_map/convert_element_type | solution.py:109
  29.3 0.1 rev.3
  29.4 0.1 reshape.208
  29.7 0.2 fusion.35
  29.8 0.2 fusion.45
  30.0 0.2 convolution_add_fusion.13
  30.2 0.2 convolution_add_fusion.12
  30.4 0.2 convolution_add_fusion.11
  30.6 0.2 convolution_add_fusion.10
  30.7 0.2 convolution_add_fusion.9
  30.9 0.2 convolution_add_fusion.8
  31.1 0.3 convolution_convert_fusion.2
  31.4 0.1 copy.19
  31.5 0.1 reshape.202
  31.7 1.8 %all_gather.3 = bf16[1,16,1024]{2,1,0:T(8,128)(2,1)S(1)} all-gather(bf16[1,8,1024]{2,1,0:T(8,128)(2,1)S(1)} %reshape.202), channel_id=1, replica_groups=mesh['tm'=16,'space'=2] {'space'}, dimensions={1}, use_global_device_ids=true | all-gather | bytes 49152 | tf_op jit(solution)/shard_map/all_gather | solution.py:120
  33.5 3.4 %collective-permute-start.2 = (bf16[1,16,1024]{2,1,0:T(8,128)(2,1)S(1)}, bf16[1,16,1024]{2,1,0:T(8,128)(2,1)S(1)}, u32[]{:S(2)}, u32[]{:S(2)}) collective-permute-start(bf16[1,16,1024]{2,1,0:T(8,128)(2,1)S(1)} %all_gather.3), channel_id=1, source_target_pairs={{0,2},{2,4},{4,6},{6,8},{8,10},{10,12},{12,14},{14,16},{16,18},{18... | collective-permute-start | bytes 98312 | tf_op jit(solution)/shard_map/ppermute | solution.py:13
  36.9 3.4 %collective-permute-start.3 = (bf16[1,16,1024]{2,1,0:T(8,128)(2,1)S(1)}, bf16[1,16,1024]{2,1,0:T(8,128)(2,1)S(1)}, u32[]{:S(2)}, u32[]{:S(2)}) collective-permute-start(bf16[1,16,1024]{2,1,0:T(8,128)(2,1)S(1)} %all_gather.3), channel_id=1, source_target_pairs={{0,4},{2,6},{4,8},{6,10},{8,12},{10,14},{12,16},{14,18},{16,20},{1... | collective-permute-start | bytes 98312 | tf_op jit(solution)/shard_map/ppermute | solution.py:13
  40.3 3.4 %collective-permute-start.4 = (bf16[1,16,1024]{2,1,0:T(8,128)(2,1)S(1)}, bf16[1,16,1024]{2,1,0:T(8,128)(2,1)S(1)}, u32[]{:S(2)}, u32[]{:S(2)}) collective-permute-start(bf16[1,16,1024]{2,1,0:T(8,128)(2,1)S(1)} %all_gather.3), channel_id=1, source_target_pairs={{0,6},{2,8},{4,10},{6,12},{8,14},{10,16},{12,18},{14,20},{16,22},{... | collective-permute-start | bytes 98312 | tf_op jit(solution)/shard_map/ppermute | solution.py:13
  43.7 0.1 reshape.207
  43.8 0.1 fusion.118
  43.9 0.1 fusion.14
  44.0 0.2 fusion.113
  44.2 0.1 convolution_convert_fusion.1
  44.4 3.5 %collective-permute-done.4 = bf16[1,16,1024]{2,1,0:T(8,128)(2,1)S(1)} collective-permute-done((bf16[1,16,1024]{2,1,0:T(8,128)(2,1)S(1)}, bf16[1,16,1024]{2,1,0:T(8,128)(2,1)S(1)}, u32[]{:S(2)}, u32[]{:S(2)}) %collective-permute-start.4) | collective-permute-done | bytes 32800 | tf_op jit(solution)/shard_map/ppermute | solution.py:13
  47.9 0.2 reshape_reshape.3
  48.1 0.2 convolution_convert_fusion
  48.3 0.1 squeeze.49
  48.4 0.4 fusion.115
  48.8 0.1 squeeze.51
  49.0 0.4 fusion.114
  49.4 0.1 squeeze.50
  49.5 0.4 fusion.116
  50.0 0.2 fusion.63
  50.3 0.2 fusion.33
  50.5 0.2 convolution_add_fusion.6
  50.7 0.2 convolution_add_fusion.5
  51.0 0.1 copy-done.2
  51.1 0.1 copy-done.5
  51.2 1.0 %fusion.13 = bf16[128,256]{1,0:T(8,128)(2,1)} fusion(bf16[256,256]{1,0:T(8,128)(2,1)S(1)} %copy-done.5, f32[128,256]{1,0:T(8,128)S(1)} %convolution_add_fusion.5, bf16[128,256]{1,0:T(8,128)(2,1)S(1)} %bitcast.109, bf16[1,256]{1,0:T(2,128)(2,1)S(1)} %convert_element_type.131, bf16[64,256]{1,0:T(8,128)(2,1)S(1)} %convolution_convert_fusion.1, ...), kind=kOutput, calls=%fused_computation.30 | convolution fusion | flops 21292416 | bytes 460800 | tf_op jit(solution)/shard_map/dot_general | solution.py:184
  (42 shorter events, 0.3 us)
Async XLA Ops:
  0.6 1.6 %copy-start = (bf16[256,256]{1,0:T(8,128)(2,1)S(1)}, bf16[256,256]{1,0:T(8,128)(2,1)}, u32[]{:S(2)}) copy-start(bf16[256,256]{1,0:T(8,128)(2,1)} %param.16) | copy-start | bytes 393220
  0.6 28.7 %copy-start.7 = (bf16[16,256]{1,0:T(8,128)(2,1)S(1)}, bf16[16,256]{1,0:T(8,128)(2,1)}, u32[]{:S(2)}) copy-start(bf16[16,256]{1,0:T(8,128)(2,1)} %param.26) | copy-start | bytes 24580
  0.7 29.0 %copy-start.3 = (bf16[3,3,256,256]{3,2,1,0:T(8,128)(2,1)S(1)}, bf16[3,3,256,256]{3,2,1,0:T(8,128)(2,1)}, u32[]{:S(2)}) copy-start(bf16[3,3,256,256]{3,2,1,0:T(8,128)(2,1)} %param.18) | copy-start | bytes 3538948
  3.3 26.2 %collective-permute-start.1 = (bf16[1,1,16,256]{3,2,1,0:T(8,128)(2,1)S(1)}, bf16[1,1,16,256]{3,2,1,0:T(8,128)(2,1)S(1)}, u32[]{:S(2)}, u32[]{:S(2)}) collective-permute-start(bf16[1,1,16,256]{3,2,1,0:T(8,128)(2,1)S(1)} %get-tuple-element.15), channel_id=1, source_target_pairs={{1,0},{3,2},{5,4},{7,6},{9,8},{11,10},{13,12},{15,14},{17,16},{19,... | collective-permute-start | bytes 24584 | tf_op jit(solution)/shard_map/ppermute | solution.py:24
  4.6 25.0 %collective-permute-start = (bf16[1,1,16,256]{3,2,1,0:T(8,128)(2,1)S(1)}, bf16[1,1,16,256]{3,2,1,0:T(8,128)(2,1)S(1)}, u32[]{:S(2)}, u32[]{:S(2)}) collective-permute-start(bf16[1,1,16,256]{3,2,1,0:T(8,128)(2,1)S(1)} %get-tuple-element.14), channel_id=1, source_target_pairs={{0,1},{2,3},{4,5},{6,7},{8,9},{10,11},{12,13},{14,15},{16,17},{18,... | collective-permute-start | bytes 24584 | tf_op jit(solution)/shard_map/ppermute | solution.py:21
  15.3 28.3 %all-to-all-start = ((bf16[16,2,128]{2,1,0:T(2,128)(2,1)}), bf16[16,2,128]{2,1,0:T(2,128)(2,1)S(1)}, u32[]{:S(2)}, u32[]{:S(2)}) async-start(bf16[16,2,128]{2,1,0:T(2,128)(2,1)} %reshape.218), calls=%async_computation | async-start | bytes 16384 | tf_op jit(solution)/shard_map/all_to_all | solution.py:111
  30.2 0.9 %copy-start.8 = (bf16[256,64]{0,1:T(8,128)(2,1)S(1)}, bf16[256,64]{0,1:T(8,128)(2,1)}, u32[]{:S(2)}) copy-start(bf16[256,64]{0,1:T(8,128)(2,1)} %param.19) | copy-start | bytes 98308
  30.5 13.3 %copy-start.1 = (bf16[64,256]{1,0:T(8,128)(2,1)S(1)}, bf16[64,256]{1,0:T(8,128)(2,1)}, u32[]{:S(2)}) copy-start(bf16[64,256]{1,0:T(8,128)(2,1)} %param.22) | copy-start | bytes 98308
  30.7 13.5 %copy-start.4 = (bf16[64,256]{1,0:T(8,128)(2,1)S(1)}, bf16[64,256]{1,0:T(8,128)(2,1)}, u32[]{:S(2)}) copy-start(bf16[64,256]{1,0:T(8,128)(2,1)} %param.23) | copy-start | bytes 98308
  31.7 17.7 %copy-start.6 = (bf16[1,8,1024]{2,1,0:T(8,128)(2,1)}, bf16[1,8,1024]{2,1,0:T(8,128)(2,1)S(1)}, u32[]{:S(2)}) copy-start(bf16[1,8,1024]{2,1,0:T(8,128)(2,1)S(1)} %reshape.202) | copy-start | bytes 49156
  33.5 10.9 %collective-permute-start.2 = (bf16[1,16,1024]{2,1,0:T(8,128)(2,1)S(1)}, bf16[1,16,1024]{2,1,0:T(8,128)(2,1)S(1)}, u32[]{:S(2)}, u32[]{:S(2)}) collective-permute-start(bf16[1,16,1024]{2,1,0:T(8,128)(2,1)S(1)} %all_gather.3), channel_id=1, source_target_pairs={{0,2},{2,4},{4,6},{6,8},{8,10},{10,12},{12,14},{14,16},{16,18},{18... | collective-permute-start | bytes 98312 | tf_op jit(solution)/shard_map/ppermute | solution.py:13
  36.9 7.5 %collective-permute-start.3 = (bf16[1,16,1024]{2,1,0:T(8,128)(2,1)S(1)}, bf16[1,16,1024]{2,1,0:T(8,128)(2,1)S(1)}, u32[]{:S(2)}, u32[]{:S(2)}) collective-permute-start(bf16[1,16,1024]{2,1,0:T(8,128)(2,1)S(1)} %all_gather.3), channel_id=1, source_target_pairs={{0,4},{2,6},{4,8},{6,10},{8,12},{10,14},{12,16},{14,18},{16,20},{1... | collective-permute-start | bytes 98312 | tf_op jit(solution)/shard_map/ppermute | solution.py:13
  40.3 7.6 %collective-permute-start.4 = (bf16[1,16,1024]{2,1,0:T(8,128)(2,1)S(1)}, bf16[1,16,1024]{2,1,0:T(8,128)(2,1)S(1)}, u32[]{:S(2)}, u32[]{:S(2)}) collective-permute-start(bf16[1,16,1024]{2,1,0:T(8,128)(2,1)S(1)} %all_gather.3), channel_id=1, source_target_pairs={{0,6},{2,8},{4,10},{6,12},{8,14},{10,16},{12,18},{14,20},{16,22},{... | collective-permute-start | bytes 98312 | tf_op jit(solution)/shard_map/ppermute | solution.py:13
  50.2 0.8 %copy-start.2 = (bf16[1,8,16,256]{3,2,1,0:T(8,128)(2,1)S(1)}, bf16[1,8,16,256]{3,2,1,0:T(8,128)(2,1)}, u32[]{:S(2)}) copy-start(bf16[1,8,16,256]{3,2,1,0:T(8,128)(2,1)} %param.14) | copy-start | bytes 196612
  50.2 0.9 %copy-start.5 = (bf16[256,256]{1,0:T(8,128)(2,1)S(1)}, bf16[256,256]{1,0:T(8,128)(2,1)}, u32[]{:S(2)}) copy-start(bf16[256,256]{1,0:T(8,128)(2,1)} %param.24) | copy-start | bytes 393220
